TPU v7x, 512 devices: a whole 4x4x16 slice. The times are simulated.
512 devices in a mesh: cp: 64 (over y, x, z_lo), sp: 8 (over z_hi, core).
Axes of the slice: x: 4, y: 4, z: 16 (z_hi: 4, z_lo: 4; z = z_hi * 4 + z_lo), core: 2. Of those that a mesh axis runs over, the one named last changes fastest.
Arguments:
- queries: bfloat16 [16384, 2048], P('cp', 'sp'), may hold values from -22 to 22
- keys: bfloat16 [16384, 128], P(('cp', 'sp')), may hold values from -5 to 5
- values: bfloat16 [16384, 128], P(('cp', 'sp')), may hold values from -6 to 6
- doc_ids: int32 [128], replicated, may hold values from 0 to 31, never falling along the last dimension, each value on 1 to 32 neighbouring positions
- span_order: int32 [64], replicated, may hold values from 0 to 63, each once
Outputs:
- attended: bfloat16 [16384, 2048], P('cp', 'sp')
Inputs may be any that keep to these rules, and one draw needn't show every extreme that they name: doc_ids never falls; each document covers 1 to 32 consecutive blocks, and one covers exactly 32. Index i of cp holds span span_order[i] of the sequence; each span once.
All inputs are finite; a program needn't handle non-finite values.
Results may differ from a plain program's by a relative error of at most 0.0036.
Values may be sent and summed in bfloat16 or wider, within the bound.
A program may use at most 64 MiB of HBM per device.

v0:
```python
import math

import jax
import jax.numpy as jnp
from jax import lax
from jax.sharding import PartitionSpec as P

HD = 128
SPAN = 256
BLK = 128


NEGATIVE = -1e30


def true_position(row_ids, span_order):
    span_index = row_ids // SPAN
    lookup = jnp.arange(span_order.shape[0], dtype=jnp.int32)
    placed = jnp.sum(
        jnp.where(span_index[:, None] == lookup[None, :], span_order[None, :], 0), axis=1
    )
    return placed * SPAN + row_ids % SPAN


def doc_lookup(position, doc_ids):
    block_index = position // BLK
    lookup = jnp.arange(doc_ids.shape[0], dtype=jnp.int32)
    return jnp.sum(jnp.where(block_index[:, None] == lookup[None, :], doc_ids[None, :], 0), axis=1)


def make_folder(query_block, query_pos, query_doc, span_order, doc_ids):
    score_scale = 1.0 / math.sqrt(query_block.shape[2])

    def fold_piece(carried, piece, start):
        key_piece, value_piece = piece
        piece_rows = key_piece.shape[0]
        tile_rows = math.gcd(piece_rows, SPAN)
        tile_count = piece_rows // tile_rows
        key_tiles = key_piece.reshape(tile_count, tile_rows, key_piece.shape[1])
        value_tiles = value_piece.reshape(tile_count, tile_rows, value_piece.shape[1])

        def tile_step(state_now, tile_inputs):
            key_tile, value_tile, tile_index = tile_inputs
            row_ids = tile_index * tile_rows + jnp.arange(tile_rows, dtype=jnp.int32)
            key_pos = true_position(row_ids, span_order)
            key_doc = doc_lookup(key_pos, doc_ids)
            allowed = (key_pos[None, :] <= query_pos[:, None]) & (
                key_doc[None, :] == query_doc[:, None]
            )
            run_max, run_total, run_accum = state_now
            scores = (
                jnp.einsum("rhd,kd->hrk", query_block, key_tile, preferred_element_type=jnp.float32)
                * score_scale
            )
            masked = jnp.where(allowed[None], scores, NEGATIVE)
            new_max = jnp.maximum(run_max, jnp.max(masked, axis=2))
            rescale = jnp.exp(run_max - new_max)
            weights = jnp.where(allowed[None], jnp.exp(masked - new_max[:, :, None]), 0.0)
            new_total = run_total * rescale + jnp.sum(weights, axis=2)
            product = jnp.einsum(
                "hrk,kd->rhd",
                weights.astype(jnp.bfloat16),
                value_tile,
                preferred_element_type=jnp.float32,
            )
            new_accum = run_accum * jnp.transpose(rescale)[:, :, None] + product
            result = (new_max, new_total, new_accum)
            return (result, None)

        tile_ids = jnp.arange(tile_count, dtype=jnp.int32)
        carried, unused = lax.scan(tile_step, carried, (key_tiles, value_tiles, tile_ids))
        return carried

    return fold_piece


def shards(queries, keys, values, doc_ids, span_order):
    cp_index = lax.axis_index("cp")
    query_ids = cp_index * SPAN + jnp.arange(queries.shape[0], dtype=jnp.int32)
    query_count = queries.shape[0]
    head_count = queries.shape[1] // HD
    query_block = queries.reshape(query_count, head_count, HD)
    query_pos = true_position(query_ids, span_order)
    query_doc = doc_lookup(query_pos, doc_ids)
    folder = make_folder(query_block, query_pos, query_doc, span_order, doc_ids)
    initial = (
        jnp.full((head_count, query_count), NEGATIVE, jnp.float32),
        jnp.zeros((head_count, query_count), jnp.float32),
        jnp.zeros((query_count, head_count, HD), jnp.float32),
    )
    group_keys, group_values = (
        lax.all_gather(keys, "sp", axis=0, tiled=True),
        lax.all_gather(values, "sp", axis=0, tiled=True),
    )
    final = folder(
        initial,
        (
            lax.all_gather(group_keys, "cp", axis=0, tiled=True),
            lax.all_gather(group_values, "cp", axis=0, tiled=True),
        ),
        jnp.int32(0),
    )
    run_max, run_total, run_accum = final
    attended = (run_accum / jnp.transpose(run_total)[:, :, None]).astype(jnp.bfloat16)
    attended = attended.reshape(query_count, head_count * HD)
    return attended


def solution(mesh):
    in_specs = (P("cp", "sp"), P(("cp", "sp"), None), P(("cp", "sp"), None), P(), P())
    out_specs = P("cp", "sp")
    return jax.shard_map(shards, mesh=mesh, in_specs=in_specs, out_specs=out_specs, check_vma=False)
```

profile of v0, /device:TPU:94, one launch (start us, length us, event | category | flops | bytes accessed | tf_op | source)
XLA Modules:
  0.0 1104.7 jit_solution(16146311559544574172)
XLA Ops:
  6.5 26.0 %all_gather.12 = bf16[256,128]{1,0:T(8,128)(2,1)} all-gather(bf16[32,128]{1,0:T(8,128)(2,1)} %param.8), channel_id=1, replica_groups=mesh['cp'=64,'sp'=8] {'sp'}, dimensions={0}, use_global_device_ids=true | all-gather | bytes 73728 | tf_op jit(solution)/shard_map/all_gather | solution.py:92
  32.6 19.5 %all_gather.14 = bf16[256,128]{1,0:T(8,128)(2,1)} all-gather(bf16[32,128]{1,0:T(8,128)(2,1)} %param.9), channel_id=1, replica_groups=mesh['cp'=64,'sp'=8] {'sp'}, dimensions={0}, use_global_device_ids=true | all-gather | bytes 73728 | tf_op jit(solution)/shard_map/all_gather | solution.py:93
  55.0 337.2 %all-gather.3.cloned.1.call-done = bf16[16384,128]{1,0:T(8,128)(2,1)} async-done(((bf16[256,128]{1,0:T(8,128)(2,1)}), bf16[16384,128]{1,0:T(8,128)(2,1)}) %all-gather.3.cloned.1.call-update) | async-done | bytes 4194320 | tf_op jit(solution)/shard_map/all_gather | solution.py:98
  392.1 362.4 %all-gather.5.cloned.1.call-done = bf16[16384,128]{1,0:T(8,128)(2,1)} async-done(((bf16[256,128]{1,0:T(8,128)(2,1)}), bf16[16384,128]{1,0:T(8,128)(2,1)}) %all-gather.5.cloned.1.call-update) | async-done | bytes 4194320 | tf_op jit(solution)/shard_map/all_gather | solution.py:99
  754.5 342.6 %while.18 = (s32[]{:T(128)}, f32[2,256]{1,0:T(2,128)S(1)}, f32[2,256]{1,0:T(2,128)S(1)}, f32[256,2,128]{0,2,1:T(8,128)S(1)}, s32[64]{0:T(128)S(1)}, /*index=5*/s...) while((s32[]{:T(128)}, f32[2,256]{1,0:T(2,128)S(1)}, ...), condition=%wide.region_7.8_spmd.clone, body=%wide.region_2.7_spmd.clone.sunk | while | flops 68843264 | bytes 2668473 | solution.py:71
  758.5 1.1 fusion.43
  763.9 1.1 fusion.43
  769.2 1.1 fusion.43
  774.6 1.1 fusion.43
  779.9 1.1 fusion.43
  785.3 1.1 fusion.43
  790.6 1.1 fusion.43
  796.0 1.1 fusion.43
  801.4 1.1 fusion.43
  806.7 1.1 fusion.43
  812.1 1.1 fusion.43
  817.4 1.1 fusion.43
  822.8 1.1 fusion.43
  828.1 1.1 fusion.43
  833.5 1.1 fusion.43
  838.8 1.1 fusion.43
  844.2 1.1 fusion.43
  849.5 1.1 fusion.43
  854.9 1.1 fusion.43
  860.2 1.1 fusion.43
  865.6 1.1 fusion.43
  870.9 1.1 fusion.43
  876.3 1.1 fusion.43
  881.7 1.1 fusion.43
  887.0 1.1 fusion.43
  892.4 1.1 fusion.43
  897.7 1.1 fusion.43
  903.1 1.1 fusion.43
  908.4 1.1 fusion.43
  913.8 1.1 fusion.43
  919.1 1.1 fusion.43
  924.5 1.1 fusion.43
  929.8 1.1 fusion.43
  935.2 1.1 fusion.43
  940.5 1.1 fusion.43
  945.9 1.1 fusion.43
  951.2 1.1 fusion.43
  956.6 1.1 fusion.43
  961.9 1.1 fusion.43
  967.3 1.1 fusion.43
  972.6 1.1 fusion.43
  978.0 1.1 fusion.43
  983.4 1.1 fusion.43
  (741 shorter events, 255.8 us)
Async XLA Ops:
  6.5 385.6 %all-gather.3.cloned.1.call-start = ((), (), s32[]{:S(2)}) async-start(), calls=%async_computation | async-start | bytes 4259840 | tf_op jit(solution)/shard_map/all_gather | solution.py:98
  32.6 721.9 %all-gather.5.cloned.1.call-start = ((), (), s32[]{:S(2)}) async-start(), calls=%async_computation.1 | async-start | bytes 4259840 | tf_op jit(solution)/shard_map/all_gather | solution.py:99
Sparse Core Ops, SparseCore 0:
  32.7 359.3 all-gather.2
  394.2 360.2 all-gather.4
where the time goes:
time: 1110 us; the launch traced here: 1100 us
  waiting for transfers between devices  700 us (63%)
  matrix products  143 us (13%)
  other arithmetic  124 us (11%)
  blocking collectives  45.5 us (4%)
  loops' own time  40.9 us (4%)
  local copies, waits for them, and re-layouts  37.8 us (3%)
  between operations  13.5 us (1%)
    all_gather x1, waiting for transfers between devices, shards(): lax.all_gather(group_values, 'cp', axis=0, tiled=True)  362 us
    all_gather x1, waiting for transfers between devices, shards(): lax.all_gather(group_keys, 'cp', axis=0, tiled=True)  337 us
    dot_general x64, matrix products, tile_step(): jnp.einsum('hrk,kd->rhd', weights.astype(jnp.bfloat16), value_tile, prefe...  73.6 us
    dot_general x64, matrix products, tile_step(): jnp.einsum('rhd,kd->hrk', query_block, key_tile, preferred_element_type=j...  69.8 us
    reduce_sum x65, other arithmetic, doc_lookup(): jnp.sum(jnp.where(block_index[:, None] == lookup[None, :], doc_ids[None,...  54.1 us
    reduce_sum x65, other arithmetic, true_position(): jnp.sum(jnp.where(span_index[:, None] == lookup[None, :], span_order[None...  48.6 us
    another operation x1, loops' own time, fold_piece(): lax.scan(tile_step, carried, (key_tiles, value_tiles, tile_ids))  40.9 us
    dynamic_slice x64, local copies, waits for them, and re-layouts, fold_piece(): lax.scan(tile_step, carried, (key_tiles, value_tiles, tile_ids))  35.8 us
  transfers between devices with their start and end apart: 2, of which 2 were waited for; matrix products, arithmetic and copies ran while one was open for 0% of the time, Pallas kernels for 0%

commit v1 on v0

v1 whole, which is shorter than its diff:
```python
import functools
import math

import jax
import jax.numpy as jnp
from jax import lax
from jax.experimental import pallas as pl
from jax.experimental.pallas import tpu as pltpu
from jax.sharding import PartitionSpec as P

HD = 128
SPAN = 256
BLK = 128
MOST = 32
REACH = MOST * BLK // SPAN + 1
NEGATIVE = -1e30


def plan(doc_ids, span_order, cp_index):
    stored = jnp.arange(span_order.shape[0], dtype=jnp.int32)
    mine = jnp.sum(jnp.where(stored == cp_index, span_order, 0))
    blocks = jnp.arange(doc_ids.shape[0], dtype=jnp.int32)
    doc_first = jnp.sum(jnp.where(blocks == 2 * mine, doc_ids, 0))
    doc_second = jnp.sum(jnp.where(blocks == 2 * mine + 1, doc_ids, 0))
    low_first = jnp.sum((doc_ids < doc_first).astype(jnp.int32)) * BLK
    low_second = jnp.sum((doc_ids < doc_second).astype(jnp.int32)) * BLK
    count = mine - low_first // SPAN + 1
    wanted = mine - jnp.arange(REACH, dtype=jnp.int32)
    places = jnp.sum(jnp.where(span_order[None, :] == wanted[:, None], stored[None, :], 0), axis=1)
    head = jnp.stack([count, mine * SPAN, low_first, low_second])
    return jnp.concatenate([head, places]).astype(jnp.int32)


def group_rows(x, fold):
    return fold(x.reshape(x.shape[0] // 8, 8, x.shape[1]), axis=0)


def attend_kernel(plan_ref, query_ref, kv_ref, out_ref, held, scores, accum, sems):
    count, first_pos = plan_ref[0], plan_ref[1]
    low_first, low_second = plan_ref[2], plan_ref[3]
    rate = math.log2(math.e) / math.sqrt(HD)

    def copy_of(step):
        rows = pl.ds(pl.multiple_of(plan_ref[4 + step] * SPAN, SPAN), SPAN)
        return pltpu.make_async_copy(kv_ref.at[rows, :], held.at[step], sems.at[step])

    def start(step, carried):
        copy_of(step).start()
        return carried

    lax.fori_loop(0, count, start, 0)
    heads = query_ref.shape[1] // HD
    query = jnp.concatenate([query_ref[:, h * HD : (h + 1) * HD] for h in range(heads)], axis=0)
    width = query.shape[0]
    column = lax.broadcasted_iota(jnp.int32, (1, width), 1) % SPAN
    low = jnp.where(column < BLK, low_first, low_second)
    key_row = lax.broadcasted_iota(jnp.int32, (SPAN, width), 0)

    def score(step):
        copy_of(step).wait()
        return lax.dot_general(
            held[step, :, :HD], query, (((1,), (1,)), ((), ())), preferred_element_type=jnp.float32
        )

    first = score(0)
    first = jnp.where((key_row <= column) & (key_row >= low - first_pos), first, NEGATIVE)
    scores[0] = first

    def score_step(step, top):
        block = score(step)
        block = jnp.where(key_row >= low - (first_pos - step * SPAN), block, NEGATIVE)
        scores[step] = block
        return jnp.maximum(top, group_rows(block, jnp.max))

    top = lax.fori_loop(1, count, score_step, group_rows(first, jnp.max))
    top = jnp.max(top, axis=0, keepdims=True)
    accum[...] = jnp.zeros_like(accum)

    def value_step(step, total):
        weights = jnp.exp2((scores[step] - top) * rate)
        accum[...] += lax.dot_general(
            held[step, :, HD:],
            weights.astype(jnp.bfloat16),
            (((0,), (0,)), ((), ())),
            preferred_element_type=jnp.float32,
        )
        return total + group_rows(weights, jnp.sum)

    total = lax.fori_loop(0, count, value_step, jnp.zeros((8, width), jnp.float32))
    result = accum[...] / jnp.sum(total, axis=0, keepdims=True)
    for h in range(heads):
        piece = result[:, h * SPAN : (h + 1) * SPAN].T
        out_ref[:, h * HD : (h + 1) * HD] = piece.astype(out_ref.dtype)


def attend(where, queries, kv):
    width = queries.shape[0] * (queries.shape[1] // HD)
    return pl.pallas_call(
        attend_kernel,
        out_shape=jax.ShapeDtypeStruct(queries.shape, jnp.bfloat16),
        in_specs=[
            pl.BlockSpec(memory_space=pltpu.SMEM),
            pl.BlockSpec(memory_space=pltpu.VMEM),
            pl.BlockSpec(memory_space=pl.ANY),
        ],
        out_specs=pl.BlockSpec(memory_space=pltpu.VMEM),
        scratch_shapes=[
            pltpu.VMEM((REACH, SPAN, 2 * HD), jnp.bfloat16),
            pltpu.VMEM((REACH, SPAN, width), jnp.float32),
            pltpu.VMEM((HD, width), jnp.float32),
            pltpu.SemaphoreType.DMA((REACH,)),
        ],
        compiler_params=pltpu.CompilerParams(vmem_limit_bytes=48 << 20),
    )(where, queries, kv)


def shards(queries, keys, values, doc_ids, span_order):
    where = plan(doc_ids, span_order, lax.axis_index("cp"))
    kv = jnp.concatenate([keys, values], axis=1)
    kv = lax.all_gather(kv, ("cp", "sp"), axis=0, tiled=True)
    return attend(where, queries, kv)


def solution(mesh):
    in_specs = (P("cp", "sp"), P(("cp", "sp"), None), P(("cp", "sp"), None), P(), P())
    out_specs = P("cp", "sp")
    return jax.shard_map(shards, mesh=mesh, in_specs=in_specs, out_specs=out_specs, check_vma=False)
```

time: 1110 us -> 860 us (0.77)
  the two profiles are of different devices: /device:TPU:94 before, /device:TPU:18 now
where the time goes in v1:
time: 860 us
  waiting for transfers between devices  825 us (96%)
  between operations  16.4 us (2%)
  Pallas kernels  10 us (1%)
    all_gather x1, waiting for transfers between devices, shards(): kv = lax.all_gather(kv, ('cp', 'sp'), axis=0, tiled=True)  825 us
  transfers between devices with their start and end apart: 1, of which 1 were waited for; matrix products, arithmetic and copies ran while one was open for 1% of the time, Pallas kernels for 0%

profile of v1, /device:TPU:18, one launch (start us, length us, event | category | flops | bytes accessed | tf_op | source)
XLA Modules:
  0.0 860.0 jit_solution(3241379910521737806)
XLA Ops:
  6.5 0.0 all-gather.2.cloned.1.call-start
  6.5 1.3 pad_maximum_fusion
  7.9 0.0 all-gather.2.cloned.1.call-update
  7.9 1.3 fusion
  9.7 1.3 fusion.3
  11.0 2.4 fusion.4
  15.9 0.6 iota_subtract_fusion
  16.4 0.8 select_reduce_fusion
  17.3 0.1 concatenate.6.plan_ref
  17.4 824.9 %all-gather.2.cloned.1.call-done.kv_ref = bf16[16384,256]{1,0:T(8,128)(2,1)} async-done(((bf16[32,256]{1,0:T(8,128)(2,1)}), bf16[16384,256]{1,0:T(8,128)(2,1)}) %all-gather.2.cloned.1.call-update) | async-done | bytes 8388624 | tf_op jit(solution)/shard_map/all_gather | solution.py:120
  842.2 0.0 copy-start
  842.2 0.9 copy-done
  843.1 10.0 %shard_map.55 = bf16[256,256]{1,0:T(8,128)(2,1)} custom-call(s32[21]{0:T(128)S(1)} %concatenate.6.plan_ref, bf16[256,256]{1,0:T(8,128)(2,1)S(1)} %copy-done, bf16[16384,256]{1,0:T(8,128)(2,1)} %all-gather.2.cloned.1.call-done.kv_ref), custom_call_target="tpu_custom_call" | custom-call | tf_op jit(solution)/shard_map/pallas_call | solution.py:98
Async XLA Ops:
  6.5 835.7 %all-gather.2.cloned.1.call-start = ((), (), s32[]{:S(2)}) async-start(), calls=%async_computation | async-start | bytes 8404992 | tf_op jit(solution)/shard_map/all_gather | solution.py:120
  842.2 0.9 copy-start
Sparse Core Ops, SparseCore 0:
  9.5 832.6 all-gather.1
